TPU v7x, 128 devices: a whole 4x4x4 slice. The times are simulated.
128 devices in a mesh: dp: 8 (over y, core), prompt: 16 (over x, z).
Axes of the slice: x: 4, y: 4, z: 4, core: 2. Of those that a mesh axis runs over, the one named last changes fastest.
Arguments:
- cand_hidden: bfloat16 [16, 8, 128, 1024], P('prompt', 'dp')
- ref_hidden: bfloat16 [32, 16, 128, 1024], P('dp', 'prompt')
- cand_ids: int32 [16, 8, 128], P('prompt', 'dp'), may hold values from 0 to 50264
- ref_ids: int32 [32, 16, 128], P('dp', 'prompt'), may hold values from 0 to 50264
- cand_len: int32 [16, 8], P('prompt', 'dp'), may hold values from 32 to 128
- reference_length: int32 [32, 16], P('dp', 'prompt'), may hold values from 32 to 128
- idf_table: float32 [50265], replicated, may hold values from 1 to 10
- up_weight: bfloat16 [1024, 4096], replicated, may hold values from -0.1875 to 0.1875
- up_bias: float32 [4096], replicated, may hold values from -3 to 3
- down_weight: bfloat16 [4096, 1024], replicated, may hold values from -0.09375 to 0.09375
- down_bias: float32 [1024], replicated, may hold values from -3 to 3
- norm_gain: float32 [1024], replicated, may hold values from 0.3 to 3
- norm_bias: float32 [1024], replicated, may hold values from -3 to 3
- pair_cand: int32 [8, 16, 32], P('dp', 'prompt'), may hold values from 0 to 7
- pair_ref: int32 [8, 16, 32], P('dp', 'prompt'), may hold values from 0 to 63
- pair_count: int32 [8, 16], P('dp', 'prompt'), may hold values from 8 to 32, as said below
Outputs:
- pair_scores: float32 [3, 8, 16, 32], P(None, 'dp', 'prompt')
- totals: float32 [3], replicated
Inputs may be any that keep to these rules, and one draw needn't show every extreme that they name: Slots from pair_count on are not live; some device has all 32 slots live.
All inputs are finite; a program needn't handle non-finite values.
Results may differ from a plain program's by a relative error of at most 0.0003.
Values may be sent and summed in bfloat16 or wider, within the bound.
No kernel may reach another device: no remote copies, remote signals or barrier semaphores. Data moves between devices by JAX's collectives and lax.ppermute only.
A program may use at most 128 MiB of HBM per device.

v0:
```python
import jax
import jax.numpy as jnp
from jax import lax
from jax.sharding import PartitionSpec as P


def encode_rows(hidden, up_weight, up_bias, down_weight, down_bias, norm_gain, norm_bias):
    preactivation_hidden = jnp.dot(hidden, up_weight, preferred_element_type=jnp.float32) + up_bias
    activated = jax.nn.gelu(preactivation_hidden, approximate=False).astype(jnp.bfloat16)
    summed = (
        hidden.astype(jnp.float32)
        + jnp.dot(activated, down_weight, preferred_element_type=jnp.float32)
        + down_bias
    )
    center = jnp.mean(summed, axis=-1, keepdims=True)
    spread = jnp.mean(jnp.square(summed - center), axis=-1, keepdims=True)
    normed = (summed - center) * lax.rsqrt(spread + 1e-05) * norm_gain + norm_bias
    magnitude = jnp.sum(jnp.square(normed), axis=-1, keepdims=True)
    return (normed * lax.rsqrt(magnitude + 1e-06)).astype(jnp.bfloat16)


def token_idf_weights(ids, lengths, idf_table):
    positions = jnp.arange(ids.shape[-1], dtype=jnp.int32)
    live_tokens = positions[None, :] < lengths[:, None]
    return jnp.where(live_tokens, jnp.take(idf_table, ids, axis=0), 0.0).astype(jnp.bfloat16)


def on_device(
    cand_hidden,
    ref_hidden,
    cand_ids,
    ref_ids,
    cand_len,
    reference_length,
    idf_table,
    up_weight,
    up_bias,
    down_weight,
    down_bias,
    norm_gain,
    norm_bias,
    pair_cand,
    pair_ref,
    pair_count,
):
    seq_len = cand_hidden.shape[2]
    width = cand_hidden.shape[3]

    def encode_side(hidden, ids, lengths):
        units = encode_rows(
            hidden.reshape(-1, width),
            up_weight,
            up_bias,
            down_weight,
            down_bias,
            norm_gain,
            norm_bias,
        )
        weights = token_idf_weights(ids.reshape(-1, seq_len), lengths.reshape(-1), idf_table)
        return (units.reshape(hidden.shape), weights.reshape(hidden.shape[:3]))

    ref_unit, ref_weight = encode_side(ref_hidden, ref_ids, reference_length)
    candidate_normalized, cand_weight = encode_side(cand_hidden, cand_ids, cand_len)
    cand_all, cand_wall = (
        lax.all_gather(candidate_normalized, "dp", axis=1, tiled=True),
        lax.all_gather(cand_weight, "dp", axis=1, tiled=True),
    )
    cand_all = cand_all.reshape(-1, seq_len, width)
    cand_wall = cand_wall.reshape(-1, seq_len)
    cand_pick = pair_cand.reshape(-1)
    slot_total = cand_pick.shape[0]
    ref_pick = pair_ref.reshape(-1)
    groups = lax.axis_size("prompt")
    ref_major = ref_pick // groups
    ref_minor = ref_pick % groups
    order = jnp.argsort(ref_minor, stable=True)
    sorted_minor = jnp.take(ref_minor, order, axis=0)
    sorted_major = jnp.take(ref_major, order, axis=0)
    sorted_cand = jnp.take(cand_pick, order, axis=0)
    paired_normalized = jnp.take(cand_all, sorted_cand, axis=0)
    pair_weight = jnp.take(cand_wall, sorted_cand, axis=0)
    initial = (
        jnp.zeros((slot_total, seq_len), jnp.float32),
        jnp.zeros((slot_total, seq_len), jnp.float32),
        jnp.zeros((slot_total, seq_len), jnp.bfloat16),
    )
    ref_all, ref_wall = (
        lax.all_gather(ref_unit, "prompt", axis=1, tiled=True),
        lax.all_gather(ref_weight, "prompt", axis=1, tiled=True),
    )
    shard_span = ref_all.shape[1]
    inside = (sorted_minor >= 0) & (sorted_minor < 0 + shard_span)
    within = sorted_major * shard_span + jnp.clip(sorted_minor - 0, 0, shard_span - 1)
    selected_normalized = jnp.take(ref_all.reshape(-1, seq_len, width), within, axis=0)
    chosen_weight = jnp.take(ref_wall.reshape(-1, seq_len), within, axis=0)
    cosine_similarity = jnp.einsum(
        "uqg,uog->uqo", paired_normalized, selected_normalized, preferred_element_type=jnp.float32
    )
    row_best = jnp.max(
        jnp.where(chosen_weight[:, None, :] > 0, cosine_similarity, -10000.0), axis=2
    )
    col_best = jnp.max(jnp.where(pair_weight[:, :, None] > 0, cosine_similarity, -10000.0), axis=1)
    keeper = inside[:, None]
    updated = []
    for stored, fresh in zip(initial, (row_best, col_best, chosen_weight)):
        updated.append(jnp.where(keeper, fresh, stored))
    row_best, col_best, ref_chosen = tuple(updated)
    cand_float = pair_weight.astype(jnp.float32)
    ref_float = ref_chosen.astype(jnp.float32)
    precision_sorted = jnp.sum(cand_float * row_best, axis=1) / jnp.sum(cand_float, axis=1)
    recall_sorted = jnp.sum(ref_float * col_best, axis=1) / jnp.sum(ref_float, axis=1)
    inverse = jnp.argsort(order)
    precision = jnp.take(precision_sorted, inverse, axis=0)
    recall = jnp.take(recall_sorted, inverse, axis=0)
    fmeasure = 2.0 * precision * recall / jnp.maximum(precision + recall, 0.7)
    live_slots = jnp.arange(slot_total, dtype=jnp.int32) < pair_count.reshape(1)
    stacked = jnp.where(live_slots[None, :], jnp.stack([precision, recall, fmeasure]), 0.0)
    score_sums, live_total = lax.psum(
        (jnp.sum(stacked, axis=1), jnp.sum(live_slots.astype(jnp.float32))), ("dp", "prompt")
    )
    return (stacked.reshape(3, 1, 1, slot_total), score_sums / live_total)


def solution(mesh):
    placed = (
        P("prompt", "dp", None, None),
        P("dp", "prompt", None, None),
        P("prompt", "dp", None),
        P("dp", "prompt", None),
        P("prompt", "dp"),
        P("dp", "prompt"),
        P(),
        P(),
        P(),
        P(),
        P(),
        P(),
        P(),
        P("dp", "prompt", None),
        P("dp", "prompt", None),
        P("dp", "prompt"),
    )
    return jax.shard_map(
        on_device,
        mesh=mesh,
        in_specs=placed,
        out_specs=(P(None, "dp", "prompt", None), P()),
        check_vma=False,
    )
```

profile of v0, /device:TPU:1, one launch (start us, length us, event | category | flops | bytes accessed | tf_op | source)
XLA Modules:
  0.0 263.4 jit_solution(12290140118969234346)
XLA Ops:
  7.2 13.2 %fusion.169 = (f32[128]{0:T(128)S(1)}, f32[128,1024]{1,0:T(8,128)S(1)}) fusion(f32[1024]{0:T(1024)} %param.30, bf16[4096,1024]{1,0:T(8,128)(2,1)} %param.29, bf16[1024,4096]{1,0:T(8,128)(2,1)} %param.27, f32[4096]{0:T(1024)} %param.28, bf16[1,1,128,1024]{3,2,1,0:T(8,128)(2,1)} %param.20), kind=kOutput, calls=%fused_computation.264 | convolution fusion | flops 2182610944 | bytes 17584640 | tf_op jit(solution)/shard_map/dot_general | solution.py:12
  21.0 0.9 multiply_convert_fusion.1
  22.2 30.3 %fusion.168 = (f32[512]{0:T(512)S(1)}, f32[512,1024]{1,0:T(8,128)S(1)}) fusion(f32[1024]{0:T(1024)S(1)} %copy-done.9, bf16[4096,1024]{1,0:T(8,128)(2,1)} %param.29, bf16[512,1024]{1,0:T(8,128)(2,1)S(1)} %bitcast.84, bf16[1024,4096]{1,0:T(8,128)(2,1)} %param.27, f32[4096]{0:T(1024)S(1)} %copy-done.8), kind=kOutput, calls=%fused_computation.263 | convolution fusion | flops 8730443776 | bytes 19945472 | tf_op jit(solution)/shard_map/dot_general | solution.py:12
  52.8 0.9 multiply_reduce_fusion
  53.8 1.5 multiply_convert_fusion
  56.6 1.1 gather_fusion
  57.8 12.1 %all_gather.12 = bf16[1,8,128]{2,0,1:T(2,128)(2,1)S(1)} all-gather(bf16[1,1,128]{2,0,1:T(2,128)(2,1)S(1)} %fusion.100), channel_id=1, replica_groups=mesh['dp'=8,'prompt'=16] {'dp'}, dimensions={1}, use_global_device_ids=true | all-gather | bytes 2304 | tf_op jit(solution)/shard_map/all_gather | solution.py:66
  69.9 1.6 sort.34
  71.5 0.7 gather_fusion.7
  72.2 0.7 gather_fusion.8
  72.9 0.7 gather_fusion.6
  73.6 3.1 %gather_fusion.2 = bf16[512]{0:T(512)(128)(2,1)S(1)} fusion(f32[50265]{0:T(1024)S(1)} %copy-done, s32[1024]{0:T(1024)S(1)} %pad_clamp_fusion.2), kind=kCustom, calls=%fused_computation.7 | custom fusion | bytes 4096 | tf_op jit(solution)/shard_map/jit(_take)/gather | solution.py:25
  76.8 20.3 %all_gather.13 = bf16[4,16,128]{2,0,1:T(4,128)(2,1)S(1)} all-gather(bf16[4,1,128]{2,0,1:T(4,128)(2,1)S(1)} %fusion.98), channel_id=1, replica_groups=mesh['dp'=8,'prompt'=16] {'prompt'}, dimensions={1}, use_global_device_ids=true | all-gather | bytes 17408 | tf_op jit(solution)/shard_map/all_gather | solution.py:89
  97.2 1.6 sort.35
  98.8 0.6 convert_reduce_fusion.2
  99.4 0.6 gather_fusion.1
  100.8 6.9 %gather_fusion.4 = bf16[32,128,1024]{2,1,0:T(8,128)(2,1)} fusion(bf16[8,128,1024]{2,1,0:T(8,128)(2,1)} %bitcast.74, s32[1024]{0:T(1024)S(1)} %get-tuple-element.39), kind=kCustom, calls=%fused_computation.9 | custom fusion | bytes 16777344 | tf_op jit(solution)/shard_map/jit(_take)/gather | solution.py:80
  107.7 62.4 %all-gather.4.cloned.1.call-done = bf16[4,16,128,1024]{3,2,1,0:T(8,128)(2,1)} async-done(((bf16[4,1,128,1024]{3,2,1,0:T(8,128)(2,1)}), bf16[4,16,128,1024]{3,2,1,0:T(8,128)(2,1)}) %all-gather.4.cloned.1.call-update) | async-done | bytes 16777232 | tf_op jit(solution)/shard_map/all_gather | solution.py:88
  170.1 10.8 %gather_fusion.5 = bf16[32,128,1024]{2,1,0:T(8,128)(2,1)} fusion(bf16[64,128,1024]{2,1,0:T(8,128)(2,1)} %bitcast.75, s32[1024]{0:T(1024)S(1)} %get-tuple-element.38), kind=kCustom, calls=%fused_computation.10 | custom fusion | bytes 16777344 | tf_op jit(solution)/shard_map/jit(_take)/gather | solution.py:94
  180.8 7.5 %select_reduce_fusion = (f32[32,128]{1,0:T(8,128)S(1)}, f32[32,128]{1,0:T(8,128)S(1)}) fusion(pred[32,128]{1,0:T(8,128)(4,1)S(1)} %broadcast_compare_fusion, pred[32,128]{1,0:T(8,128)(4,1)S(1)} %broadcast_compare_fusion.1, bf16[32,128,1024]{2,1,0:T(8,128)(2,1)} %gather_fusion.5, pred[32]{0:T(512)(128)(4,1)S(1)} %get-tuple-element.22, ...), kind=kOutput, calls=%fused_computation.73 | convolution fusion | flops 1084219392 | bytes 16818240 | tf_op jit(solution)/shard_map/uqg,uog->uqo/dot_general | solution.py:96
  188.6 0.7 gather_fusion.9
  189.3 0.7 gather_fusion.10
  190.2 64.7 %all-reduce = (f32[3]{0:T(128)S(1)}, f32[]{:T(128)}) all-reduce(f32[3]{0:T(128)S(1)} %fusion.96, f32[]{:T(128)} %convert_reduce_fusion.2), channel_id=1, replica_groups=mesh['dp'=8,'prompt'=16] {'dp','prompt'}, use_global_device_ids=true, to_apply=%region_15.18 | all-reduce | flops 4 | bytes 32 | tf_op jit(solution)/shard_map/psum | solution.py:118
  254.9 1.2 broadcast_divide_fusion
  (65 shorter events, 3.1 us)
Async XLA Ops:
  7.2 49.4 %copy-start = (f32[50265]{0:T(1024)S(1)}, f32[50265]{0:T(1024)}, u32[]{:S(2)}) copy-start(f32[50265]{0:T(1024)} %param.26) | copy-start | bytes 603184
  7.2 13.5 %copy-start.2 = (f32[1024]{0:T(1024)S(1)}, f32[1024]{0:T(1024)}, u32[]{:S(2)}) copy-start(f32[1024]{0:T(1024)} %param.32) | copy-start | bytes 12292
  7.2 13.5 %copy-start.3 = (f32[1024]{0:T(1024)S(1)}, f32[1024]{0:T(1024)}, u32[]{:S(2)}) copy-start(f32[1024]{0:T(1024)} %param.31) | copy-start | bytes 12292
  7.2 93.6 %all-gather.6.cloned.1.call-start = ((), (), s32[]{:S(2)}) async-start(), calls=%async_computation.1 | async-start | bytes 2359296 | tf_op jit(solution)/shard_map/all_gather | solution.py:65
  20.5 1.7 copy-start.7
  20.5 1.7 copy-start.8
  20.5 1.7 copy-start.9
  21.9 148.1 %all-gather.4.cloned.1.call-start = ((), (), s32[]{:S(2)}) async-start(), calls=%async_computation | async-start | bytes 17825792 | tf_op jit(solution)/shard_map/all_gather | solution.py:88
  53.7 2.8 %copy-start.6 = (s32[1,1,128]{2,1,0:T(1,128)S(1)}, s32[1,1,128]{2,1,0:T(1,128)}, u32[]{:S(2)}) copy-start(s32[1,1,128]{2,1,0:T(1,128)} %param.22) | copy-start | bytes 1540
  53.7 16.1 %copy-start.10 = (s32[1,1,32]{2,1,0:T(1,128)S(1)}, s32[1,1,32]{2,1,0:T(1,128)}, u32[]{:S(2)}) copy-start(s32[1,1,32]{2,1,0:T(1,128)} %param.34) | copy-start | bytes 388
  55.2 17.7 %copy-start.1 = (s32[1,1,32]{2,1,0:T(1,128)S(1)}, s32[1,1,32]{2,1,0:T(1,128)}, u32[]{:S(2)}) copy-start(s32[1,1,32]{2,1,0:T(1,128)} %param.33) | copy-start | bytes 388
  55.2 18.4 %copy-start.4 = (s32[4,1,128]{2,1,0:T(1,128)S(1)}, s32[4,1,128]{2,1,0:T(1,128)}, u32[]{:S(2)}) copy-start(s32[4,1,128]{2,1,0:T(1,128)} %param.23) | copy-start | bytes 6148
  55.2 21.6 %copy-start.5 = (s32[4,1]{0,1:T(1,128)S(1)}, s32[4,1]{0,1:T(1,128)}, u32[]{:S(2)}) copy-start(s32[4,1]{0,1:T(1,128)} %param.25) | copy-start | bytes 52
Sparse Core Ops, SparseCore 0:
  22.0 28.8 all-gather.5
  55.4 114.6 all-gather.3
where the time goes:
time: 264 us; the launch traced here: 263 us
  blocking collectives  97 us (37%)
  waiting for transfers between devices  62.4 us (24%)
  matrix products  51 us (19%)
  local copies, waits for them, and re-layouts  26.7 us (10%)
  between operations  15.6 us (6%)
  other arithmetic  10.3 us (4%)
    psum x1, blocking collectives, on_device(): lax.psum((jnp.sum(stacked, axis=1), jnp.sum(live_slots.astype(jnp.float32...  64.7 us
    all_gather x1, waiting for transfers between devices, on_device(): lax.all_gather(ref_unit, 'prompt', axis=1, tiled=True)  62.4 us
    dot_general x2, matrix products, encode_rows(): jnp.dot(activated, down_weight, preferred_element_type=jnp.float32)  43.5 us
    all_gather x1, blocking collectives, on_device(): lax.all_gather(ref_weight, 'prompt', axis=1, tiled=True)  20.3 us
    all_gather x1, blocking collectives, on_device(): lax.all_gather(cand_weight, 'dp', axis=1, tiled=True)  12.1 us
    gather x1, local copies, waits for them, and re-layouts, on_device(): jnp.take(ref_all.reshape(-1, seq_len, width), within, axis=0)  10.8 us
    dot_general x1, matrix products, on_device(): jnp.einsum('uqg,uog->uqo', paired_normalized, selected_normalized, prefer...  7.55 us
    gather x1, local copies, waits for them, and re-layouts, on_device(): paired_normalized = jnp.take(cand_all, sorted_cand, axis=0)  6.87 us
  transfers between devices with their start and end apart: 2, of which 1 were waited for; matrix products, arithmetic and copies ran while one was open for 20% of the time, Pallas kernels for 0%

commit v1 on v0

--- a/solution.py
+++ b/solution.py
@@ -115,8 +115,11 @@
     fmeasure = 2.0 * precision * recall / jnp.maximum(precision + recall, 0.7)
     live_slots = jnp.arange(slot_total, dtype=jnp.int32) < pair_count.reshape(1)
     stacked = jnp.where(live_slots[None, :], jnp.stack([precision, recall, fmeasure]), 0.0)
-    score_sums, live_total = lax.psum(
-        (jnp.sum(stacked, axis=1), jnp.sum(live_slots.astype(jnp.float32))), ("dp", "prompt")
+    create_the_rails = lambda content, along_axis, across: lax.psum(
+        lax.psum(content, along_axis), across
+    )
+    score_sums, live_total = create_the_rails(
+        (jnp.sum(stacked, axis=1), jnp.sum(live_slots.astype(jnp.float32))), "dp", across="prompt"
     )
     return (stacked.reshape(3, 1, 1, slot_total), score_sums / live_total)
 

time: 264 us -> 253 us (0.958)
  the two profiles are of different devices: /device:TPU:1 before, /device:TPU:0 now
where the time goes in v1:
time: 253 us; the launch traced here: 252 us
  blocking collectives  89.8 us (35%)
  waiting for transfers between devices  58.8 us (23%)
  matrix products  51 us (20%)
  local copies, waits for them, and re-layouts  26.5 us (10%)
  between operations  15.6 us (6%)
  other arithmetic  10.3 us (4%)
    all_gather x1, waiting for transfers between devices, on_device(): lax.all_gather(ref_unit, 'prompt', axis=1, tiled=True)  58.7 us
    dot_general x2, matrix products, encode_rows(): jnp.dot(activated, down_weight, preferred_element_type=jnp.float32)  43.5 us
    psum x1, blocking collectives, on_device(): lax.psum(lax.psum(content, along_axis), across)  39.5 us
    all_gather x1, blocking collectives, on_device(): lax.all_gather(ref_weight, 'prompt', axis=1, tiled=True)  24.6 us
    psum x1, blocking collectives, on_device(): lax.psum(content, along_axis)  14.8 us
    all_gather x1, blocking collectives, on_device(): lax.all_gather(cand_weight, 'dp', axis=1, tiled=True)  10.8 us
    gather x1, local copies, waits for them, and re-layouts, on_device(): jnp.take(ref_all.reshape(-1, seq_len, width), within, axis=0)  10.8 us
    dot_general x1, matrix products, on_device(): jnp.einsum('uqg,uog->uqo', paired_normalized, selected_normalized, prefer...  7.55 us
  transfers between devices with their start and end apart: 2, of which 1 were waited for; matrix products, arithmetic and copies ran while one was open for 20% of the time, Pallas kernels for 0%

profile of v1, /device:TPU:0, one launch (start us, length us, event | category | flops | bytes accessed | tf_op | source)
XLA Modules:
  0.0 252.3 jit_solution(9200794824276743782)
XLA Ops:
  7.2 13.2 %fusion.169 = (f32[128]{0:T(128)S(1)}, f32[128,1024]{1,0:T(8,128)S(1)}) fusion(f32[1024]{0:T(1024)} %param.30, bf16[4096,1024]{1,0:T(8,128)(2,1)} %param.29, bf16[1024,4096]{1,0:T(8,128)(2,1)} %param.27, f32[4096]{0:T(1024)} %param.28, bf16[1,1,128,1024]{3,2,1,0:T(8,128)(2,1)} %param.20), kind=kOutput, calls=%fused_computation.264 | convolution fusion | flops 2182610944 | bytes 17584640 | tf_op jit(solution)/shard_map/dot_general | solution.py:12
  21.0 0.9 multiply_convert_fusion.1
  22.2 30.3 %fusion.168 = (f32[512]{0:T(512)S(1)}, f32[512,1024]{1,0:T(8,128)S(1)}) fusion(f32[1024]{0:T(1024)S(1)} %copy-done.9, bf16[4096,1024]{1,0:T(8,128)(2,1)} %param.29, bf16[512,1024]{1,0:T(8,128)(2,1)S(1)} %bitcast.84, bf16[1024,4096]{1,0:T(8,128)(2,1)} %param.27, f32[4096]{0:T(1024)S(1)} %copy-done.8), kind=kOutput, calls=%fused_computation.263 | convolution fusion | flops 8730443776 | bytes 19945472 | tf_op jit(solution)/shard_map/dot_general | solution.py:12
  52.8 0.9 multiply_reduce_fusion
  53.7 1.5 multiply_convert_fusion
  56.6 1.1 gather_fusion
  57.8 10.8 %all_gather.12 = bf16[1,8,128]{2,0,1:T(2,128)(2,1)S(1)} all-gather(bf16[1,1,128]{2,0,1:T(2,128)(2,1)S(1)} %fusion.100), channel_id=1, replica_groups=mesh['dp'=8,'prompt'=16] {'dp'}, dimensions={1}, use_global_device_ids=true | all-gather | bytes 2304 | tf_op jit(solution)/shard_map/all_gather | solution.py:66
  68.6 1.6 sort.34
  70.2 0.7 gather_fusion.7
  70.9 0.7 gather_fusion.8
  71.6 0.7 gather_fusion.6
  72.4 3.1 %gather_fusion.2 = bf16[512]{0:T(512)(128)(2,1)S(1)} fusion(f32[50265]{0:T(1024)S(1)} %copy-done, s32[1024]{0:T(1024)S(1)} %pad_clamp_fusion.2), kind=kCustom, calls=%fused_computation.7 | custom fusion | bytes 4096 | tf_op jit(solution)/shard_map/jit(_take)/gather | solution.py:25
  75.6 24.6 %all_gather.13 = bf16[4,16,128]{2,0,1:T(4,128)(2,1)S(1)} all-gather(bf16[4,1,128]{2,0,1:T(4,128)(2,1)S(1)} %fusion.98), channel_id=1, replica_groups=mesh['dp'=8,'prompt'=16] {'prompt'}, dimensions={1}, use_global_device_ids=true | all-gather | bytes 17408 | tf_op jit(solution)/shard_map/all_gather | solution.py:89
  100.2 1.6 sort.35
  101.8 0.6 convert_reduce_fusion.2
  103.9 6.7 %gather_fusion.4 = bf16[32,128,1024]{2,1,0:T(8,128)(2,1)} fusion(bf16[8,128,1024]{2,1,0:T(8,128)(2,1)} %bitcast.74, s32[1024]{0:T(1024)S(1)} %get-tuple-element.41), kind=kCustom, calls=%fused_computation.9 | custom fusion | bytes 16777344 | tf_op jit(solution)/shard_map/jit(_take)/gather | solution.py:80
  110.6 58.7 %all-gather.4.cloned.1.call-done = bf16[4,16,128,1024]{3,2,1,0:T(8,128)(2,1)} async-done(((bf16[4,1,128,1024]{3,2,1,0:T(8,128)(2,1)}), bf16[4,16,128,1024]{3,2,1,0:T(8,128)(2,1)}) %all-gather.4.cloned.1.call-update) | async-done | bytes 16777232 | tf_op jit(solution)/shard_map/all_gather | solution.py:88
  169.3 10.8 %gather_fusion.5 = bf16[32,128,1024]{2,1,0:T(8,128)(2,1)} fusion(bf16[64,128,1024]{2,1,0:T(8,128)(2,1)} %bitcast.75, s32[1024]{0:T(1024)S(1)} %get-tuple-element.40), kind=kCustom, calls=%fused_computation.10 | custom fusion | bytes 16777344 | tf_op jit(solution)/shard_map/jit(_take)/gather | solution.py:94
  180.1 7.5 %select_reduce_fusion = (f32[32,128]{1,0:T(8,128)S(1)}, f32[32,128]{1,0:T(8,128)S(1)}) fusion(pred[32,128]{1,0:T(8,128)(4,1)S(1)} %broadcast_compare_fusion, pred[32,128]{1,0:T(8,128)(4,1)S(1)} %broadcast_compare_fusion.1, bf16[32,128,1024]{2,1,0:T(8,128)(2,1)} %gather_fusion.5, pred[32]{0:T(512)(128)(4,1)S(1)} %get-tuple-element.24, ...), kind=kOutput, calls=%fused_computation.73 | convolution fusion | flops 1084219392 | bytes 16818240 | tf_op jit(solution)/shard_map/uqg,uog->uqo/dot_general | solution.py:96
  187.9 0.7 gather_fusion.9
  188.6 0.7 gather_fusion.10
  189.4 14.8 %all-reduce.1 = (f32[3]{0:T(128)S(1)}, f32[]{:T(128)}) all-reduce(f32[3]{0:T(128)S(1)} %fusion.96, f32[]{:T(128)} %convert_reduce_fusion.2), channel_id=1, replica_groups=mesh['dp'=8,'prompt'=16] {'dp'}, use_global_device_ids=true, to_apply=%region_15.18 | all-reduce | flops 4 | bytes 32 | tf_op jit(solution)/shard_map/psum | solution.py:119
  204.2 39.5 %all-reduce = (f32[3]{0:T(128)S(1)}, f32[]{:T(128)}) all-reduce(f32[3]{0:T(128)S(1)} %get-tuple-element.18, f32[]{:T(128)} %get-tuple-element.19), channel_id=1, replica_groups=mesh['dp'=8,'prompt'=16] {'prompt'}, use_global_device_ids=true, to_apply=%region_16.19 | all-reduce | flops 4 | bytes 32 | tf_op jit(solution)/shard_map/psum | solution.py:118
  243.7 1.2 broadcast_divide_fusion
  (66 shorter events, 3.7 us)
Async XLA Ops:
  7.2 49.4 %copy-start = (f32[50265]{0:T(1024)S(1)}, f32[50265]{0:T(1024)}, u32[]{:S(2)}) copy-start(f32[50265]{0:T(1024)} %param.26) | copy-start | bytes 603184
  7.2 13.5 %copy-start.2 = (f32[1024]{0:T(1024)S(1)}, f32[1024]{0:T(1024)}, u32[]{:S(2)}) copy-start(f32[1024]{0:T(1024)} %param.32) | copy-start | bytes 12292
  7.2 13.5 %copy-start.3 = (f32[1024]{0:T(1024)S(1)}, f32[1024]{0:T(1024)}, u32[]{:S(2)}) copy-start(f32[1024]{0:T(1024)} %param.31) | copy-start | bytes 12292
  7.2 96.7 %all-gather.6.cloned.1.call-start = ((), (), s32[]{:S(2)}) async-start(), calls=%async_computation.1 | async-start | bytes 2359296 | tf_op jit(solution)/shard_map/all_gather | solution.py:65
  20.5 1.7 copy-start.7
  20.5 1.7 copy-start.8
  20.5 1.7 copy-start.9
  21.9 147.4 %all-gather.4.cloned.1.call-start = ((), (), s32[]{:S(2)}) async-start(), calls=%async_computation | async-start | bytes 17825792 | tf_op jit(solution)/shard_map/all_gather | solution.py:88
  53.7 2.8 %copy-start.6 = (s32[1,1,128]{2,1,0:T(1,128)S(1)}, s32[1,1,128]{2,1,0:T(1,128)}, u32[]{:S(2)}) copy-start(s32[1,1,128]{2,1,0:T(1,128)} %param.22) | copy-start | bytes 1540
  53.7 14.9 %copy-start.10 = (s32[1,1,32]{2,1,0:T(1,128)S(1)}, s32[1,1,32]{2,1,0:T(1,128)}, u32[]{:S(2)}) copy-start(s32[1,1,32]{2,1,0:T(1,128)} %param.34) | copy-start | bytes 388
  55.2 16.5 %copy-start.1 = (s32[1,1,32]{2,1,0:T(1,128)S(1)}, s32[1,1,32]{2,1,0:T(1,128)}, u32[]{:S(2)}) copy-start(s32[1,1,32]{2,1,0:T(1,128)} %param.33) | copy-start | bytes 388
  55.2 17.2 %copy-start.4 = (s32[4,1,128]{2,1,0:T(1,128)S(1)}, s32[4,1,128]{2,1,0:T(1,128)}, u32[]{:S(2)}) copy-start(s32[4,1,128]{2,1,0:T(1,128)} %param.23) | copy-start | bytes 6148
  55.2 20.3 %copy-start.5 = (s32[4,1]{0,1:T(1,128)S(1)}, s32[4,1]{0,1:T(1,128)}, u32[]{:S(2)}) copy-start(s32[4,1]{0,1:T(1,128)} %param.25) | copy-start | bytes 52
Sparse Core Ops, SparseCore 0:
  22.0 27.6 all-gather.5
  55.3 113.9 all-gather.3
